TPU v7x, 128 devices: a whole 4x4x4 slice. The times are simulated.
128 devices in a mesh: seq: 32 (over z, y, core), head: 4 (over x).
Axes of the slice: x: 4, y: 4, z: 4, core: 2. Of those that a mesh axis runs over, the one named last changes fastest.
Arguments:
- tokens: bfloat16 [65536, 1024], P(('seq', 'head')), may hold values from -6 to 6
- w_gate_x: bfloat16 [1024, 4096], replicated, may hold values from -0.1875 to 0.1875
- w_bc_dt: bfloat16 [1024, 160], replicated, may hold values from -0.1875 to 0.1875
- conv_x_weight: float32 [4, 2048], P(None, 'head'), may hold values from -0.5 to 0.5
- conv_x_bias: float32 [2048], P('head'), may hold values from -0.5 to 0.5
- conv_bc_weight: float32 [4, 128], replicated, may hold values from -0.5 to 0.5
- conv_bc_bias: float32 [128], replicated, may hold values from -0.5 to 0.5
- dt_bias: float32 [32], P('head'), may hold values from -9 to -1
- a_log: float32 [32], P('head'), may hold values from -4 to 1
- skip_d: float32 [32], P('head'), may hold values from 0.5 to 1.5
- norm_gain: float32 [2048], replicated, may hold values from 0.1 to 1.9
- w_out: bfloat16 [2048, 1024], replicated, may hold values from -0.125 to 0.125
Outputs:
- mixed: bfloat16 [65536, 1024], P(('seq', 'head'))
All inputs are finite; a program needn't handle non-finite values.
Results may differ from a plain program's by a relative error of at most 0.009.
Values may be sent and summed in bfloat16 or wider, within the bound.
No kernel may reach another device: no remote copies, remote signals or barrier semaphores. Data moves between devices by JAX's collectives and lax.ppermute only.
A program may use at most 128 MiB of HBM per device.

v0:
```python
import jax
import jax.numpy as jnp
from jax import lax
from jax.sharding import PartitionSpec as P

HEADS = 32
HEAD_DIM = 64
STATE = 64
GROUP = 256
CONV = 4
epsilon = 1e-05


def from_behind(array, axis, by):
    size = lax.axis_size(axis)
    pairs = [(i, i + by) for i in range(size) if 0 <= i + by < size]
    return lax.ppermute(array, axis, pairs)


def prefix(array, axis, combine, identity):
    size, mine = (lax.axis_size(axis), lax.axis_index(axis))
    everything = jax.tree.map(lambda part: lax.all_gather(part, axis), array)
    start = jax.tree.map(
        lambda part, zero: jnp.broadcast_to(jnp.asarray(zero, part.dtype), part.shape),
        array,
        identity,
    )

    def hop(k, before):
        reached = k < mine
        new = combine(before, jax.tree.map(lambda part: part[k], everything))
        return jax.tree.map(lambda a, b: jnp.where(reached, a, b), new, before)

    return lax.fori_loop(0, size, hop, start)


def causal_taps(padded, weights, biases, count):
    summed = biases + weights[0] * padded[0:count]
    for tap_index in range(1, CONV):
        summed = summed + weights[tap_index] * padded[tap_index : tap_index + count]
    return jax.nn.silu(summed).astype(jnp.bfloat16)


def on_device(
    tokens,
    w_gate_x,
    w_bc_dt,
    conv_x_weight,
    conv_x_bias,
    conv_bc_weight,
    conv_bc_bias,
    dt_bias,
    a_log,
    skip_d,
    norm_gain,
    w_out,
):
    highest = lax.Precision.HIGHEST
    heads_here = dt_bias.shape[0]
    dinner_here = heads_here * HEAD_DIM
    tok_rows = tokens.shape[0]
    gate_all = jnp.dot(tokens, w_gate_x, preferred_element_type=jnp.float32).astype(jnp.bfloat16)
    gate_all = gate_all.reshape(tok_rows, HEADS, 2 * HEAD_DIM)
    bc_dt = jnp.dot(tokens, w_bc_dt, preferred_element_type=jnp.float32).astype(jnp.bfloat16)
    dt_all = bc_dt[:, 2 * STATE :].reshape(tok_rows, HEADS, 1)
    gate_x, dt_raw = (
        lax.all_to_all(gate_all, "head", split_axis=1, concat_axis=0, tiled=True),
        lax.all_to_all(dt_all, "head", split_axis=1, concat_axis=0, tiled=True),
    )
    dt_raw = dt_raw[:, :, 0]
    bc_rows = lax.all_gather(bc_dt[:, : 2 * STATE], "head", axis=0, tiled=True)
    seq_rows = gate_x.shape[0]
    gate_z = gate_x[:, :, :HEAD_DIM]
    x_chan = gate_x[:, :, HEAD_DIM:].reshape(seq_rows, dinner_here)
    conv_input = jnp.concatenate([x_chan, bc_rows], axis=1)
    rim_rows = from_behind(conv_input[seq_rows - (CONV - 1) :], "seq", 1)
    padded = jnp.concatenate([rim_rows, conv_input], axis=0).astype(jnp.float32)
    conv_weights = jnp.concatenate([conv_x_weight, conv_bc_weight], axis=1)
    conv_biases = jnp.concatenate([conv_x_bias, conv_bc_bias], axis=0)
    conved = causal_taps(padded, conv_weights, conv_biases, seq_rows)
    x_heads = conved[:, :dinner_here].astype(jnp.float32).reshape(seq_rows, heads_here, HEAD_DIM)
    b_mat = conved[:, dinner_here : dinner_here + STATE].astype(jnp.float32)
    c_mat = conved[:, dinner_here + STATE :].astype(jnp.float32)
    dt_step = jax.nn.softplus(dt_raw.astype(jnp.float32) + dt_bias)
    log_decay = dt_step * -jnp.exp(a_log)
    x_dt = x_heads * dt_step[:, :, None]
    blocks = seq_rows // GROUP
    decay_blocks = log_decay.reshape(blocks, GROUP, heads_here)
    xdt_blocks = x_dt.reshape(blocks, GROUP, heads_here, HEAD_DIM)
    b_blocks = b_mat.reshape(blocks, GROUP, STATE)
    c_blocks = c_mat.reshape(blocks, GROUP, STATE)
    cumlog = jnp.cumsum(decay_blocks, axis=1)
    scores = jnp.einsum("ktn,ksn->kts", c_blocks, b_blocks, precision=highest)
    by_head = jnp.swapaxes(cumlog, 1, 2)
    gaps = by_head[:, :, :, None] - by_head[:, :, None, :]
    causal = jnp.arange(GROUP)[:, None] >= jnp.arange(GROUP)[None, :]
    decays = jnp.where(causal[None, None], jnp.exp(jnp.minimum(gaps, 0.0)), 0.0)
    mixed = scores[:, None] * decays
    y_intra = jnp.einsum("khts,kshp->kthp", mixed, xdt_blocks, precision=highest)
    block_ends = cumlog[:, -1, :]
    to_end = jnp.exp(block_ends[:, None, :] - cumlog)
    local_states = jnp.einsum(
        "kshp,ksn->khpn", to_end[..., None] * xdt_blocks, b_blocks, precision=highest
    )

    def chain_step(carried, inputs):
        block_decay, fresh = inputs
        return (block_decay[:, None, None] * carried + fresh, carried)

    zero_state = jnp.zeros((heads_here, HEAD_DIM, STATE), jnp.float32)
    device_state, block_starts = lax.scan(
        chain_step, zero_state, (jnp.exp(block_ends), local_states)
    )
    total_log = jnp.sum(block_ends, axis=0)

    def combine(earlier, latter):
        return (earlier[0] + latter[0], earlier[1] * jnp.exp(latter[0])[:, None, None] + latter[1])

    prefix_log, incoming = prefix(
        (total_log, device_state), "seq", combine, (jnp.zeros_like(total_log), zero_state)
    )
    offset = jnp.cumsum(block_ends, axis=0) - block_ends
    start_states = block_starts + jnp.exp(offset)[:, :, None, None] * incoming[None]
    y_state = jnp.exp(cumlog)[..., None] * jnp.einsum(
        "ktn,khpn->kthp", c_blocks, start_states, precision=highest
    )
    y_heads = (y_intra + y_state).reshape(seq_rows, heads_here, HEAD_DIM) + skip_d[
        None, :, None
    ] * x_heads
    gated_out = (
        (y_heads * jax.nn.silu(gate_z.astype(jnp.float32)))
        .astype(jnp.bfloat16)
        .reshape(seq_rows, dinner_here)
    )
    by_token = lax.all_to_all(gated_out, "head", split_axis=0, concat_axis=1, tiled=True)
    gated_f = by_token.astype(jnp.float32)
    mean_sq = jnp.mean(gated_f * gated_f, axis=1, keepdims=True)
    normed = (gated_f * lax.rsqrt(mean_sq + epsilon) * norm_gain).astype(jnp.bfloat16)
    return jnp.dot(normed, w_out, preferred_element_type=jnp.float32).astype(jnp.bfloat16)


def solution(mesh):
    return jax.shard_map(
        on_device,
        mesh=mesh,
        in_specs=(
            P(("seq", "head"), None),
            P(),
            P(),
            P(None, "head"),
            P("head"),
            P(),
            P(),
            P("head"),
            P("head"),
            P("head"),
            P(),
            P(),
        ),
        out_specs=P(("seq", "head"), None),
        check_vma=False,
    )
```

profile of v0, /device:TPU:0, one launch (start us, length us, event | category | flops | bytes accessed | tf_op | source)
XLA Modules:
  0.0 321.6 jit_solution(6159652783522887039)
XLA Ops:
  6.5 1.2 copy-done
  7.8 1.5 convolution_convert_fusion.2
  9.8 0.8 reduce.13
  11.3 4.4 %all-to-all-start.1 = ((bf16[4,2,2048]{2,1,0:T(2,128)(2,1)}), bf16[4,2,2048]{2,1,0:T(2,128)(2,1)S(1)}, u32[]{:S(2)}, u32[]{:S(2)}) async-start(bf16[4,2,2048]{2,1,0:T(2,128)(2,1)} %reshape.184), calls=%async_computation.1 | async-start | bytes 65536 | tf_op jit(solution)/shard_map/all_to_all | solution.py:68
  15.7 8.1 %fusion.28 = bf16[64,32,8,128]{3,2,1,0:T(8,128)(2,1)S(1)} fusion(bf16[512,1024]{1,0:T(8,128)(2,1)S(1)} %copy-done, bf16[1024,4096]{1,0:T(8,128)(2,1)} %param.17), kind=kOutput, calls=%fused_computation.46 | convolution fusion | flops 4297064448 | bytes 13631488 | tf_op jit(solution)/shard_map/dot_general | solution.py:62
  23.8 3.1 copy.123
  27.0 5.0 %all-to-all-start = ((bf16[512,32,128]{2,0,1:T(8,128)(2,1)}), bf16[512,32,128]{2,0,1:T(8,128)(2,1)}, u32[]{:S(2)}, u32[]{:S(2)}) async-start(bf16[512,32,128]{2,0,1:T(8,128)(2,1)} %bitcast.113), calls=%async_computation | async-start | bytes 8388608 | tf_op jit(solution)/shard_map/all_to_all | solution.py:67
  32.2 56.7 %all_gather.15 = bf16[2048,128]{0,1:T(8,128)(2,1)S(1)} all-gather(bf16[512,128]{0,1:T(8,128)(2,1)S(1)} %slice.78), channel_id=1, replica_groups=mesh['seq'=32,'head'=4] {'head'}, dimensions={0}, use_global_device_ids=true | all-gather | bytes 655360 | tf_op jit(solution)/shard_map/all_gather | solution.py:71
  89.1 4.5 %reduce-window.6 = f32[8,8,2,128]{3,1,2,0:T(8,128)S(1)} reduce-window(f32[8,8,2,128]{3,1,2,0:T(8,128)S(1)} %get-tuple-element.196, f32[]{:T(128)} %constant.58.clone.1), window={size=1x1x1x128 pad=0_0x0_0x0_0x127_0}, to_apply=%region_0.1 | reduce-window | flops 2080768 | bytes 131076 | tf_op jit(solution)/shard_map/reduce-window
  94.4 4.9 %copy.73 = bf16[4,512,8,128]{3,2,1,0:T(8,128)(2,1)S(1)} copy(bf16[4,512,8,128]{3,1,2,0:T(8,128)(2,1)} %bitcast.2) | data formatting | bytes 8388608 | tf_op jit(solution)/shard_map/all_to_all | solution.py:67
  99.3 4.0 %fusion.44 = (bf16[2048,8,64]{2,1,0:T(8,128)(2,1)}, bf16[2048,8,64]{2,1,0:T(8,128)(2,1)}) fusion(bf16[2048,8,128]{2,1,0:T(8,128)(2,1)S(1)} %bitcast.109), kind=kLoop, calls=%fused_computation.87 | loop fusion | bytes 8388608 | tf_op jit(solution)/shard_map/slice | solution.py:74
  103.3 4.5 %copy.74 = bf16[2048,8,64]{0,2,1:T(8,128)(2,1)S(1)} copy(bf16[2048,8,64]{2,1,0:T(8,128)(2,1)} %get-tuple-element.198) | data formatting | bytes 4194304 | tf_op jit(solution)/shard_map/slice | solution.py:74
  107.8 1.5 collective-permute-start
  109.4 0.7 collective-permute-done
  110.2 1.1 maximum_convert_fusion
  111.3 5.2 %multiply_convert_fusion = bf16[2048,640]{0,1:T(8,128)(2,1)S(1)} fusion(f32[2051,640]{0,1:T(8,128)S(1)} %maximum_convert_fusion, f32[640]{0:T(1024)S(1)} %get-tuple-element.169, f32[640]{0:T(1024)S(1)} %get-tuple-element.170, f32[640]{0:T(1024)S(1)} %get-tuple-element.171, f32[640]{0:T(1024)S(1)} %get-tuple-element.168, f32[640]{0:T(1024)S(1)} %pad_maximum_fusion.1), kind=kLoop, calls=%fused_computation.29 | loop fusion | flops 17039360 | bytes 23605760 | tf_op jit(solution)/shard_map/convert_element_type | solution.py:41
  117.1 2.0 copy.102
  119.6 2.5 broadcast_multiply_fusion
  122.1 3.0 fusion.24
  125.2 6.8 %while.27 = (s32[]{:T(128)}, f32[8,64,64]{2,1,0:T(8,128)S(1)}, f32[8,8,64,64]{3,2,1,0:T(8,128)}, f32[8,8]{1,0:T(8,128)S(1)}, f32[8,8,64,64]{3,2,1,0:T(8,128)S(1)}, /*index=5*/s32[]{:T(128)}, s32[]{:T(128)}) while((s32[]{:T(128)}, f32[8,64,64]{2,1,0:T(8,128)S(1)}, f32[8,8,64,64]{3,2,1,0:T(8,128)}, f32[8,8]{1,0:T(8,128)S(1)}, ...), condition=%wide.region_3.4_spmd.clone, body=%wide.region_2.3_spmd.clone.sunk | while | flops 131075 | bytes 786636 | solution.py:111
  127.7 0.7 bitcast_dynamic-update-slice_fusion.2
  134.3 70.5 %all-reduce = f32[256]{0:T(256)S(1)} all-reduce(f32[256]{0:T(256)S(1)} %dynamic-update-slice), channel_id=2, replica_groups=mesh['seq'=32,'head'=4] {'seq'}, use_global_device_ids=true, to_apply=%add | all-reduce | flops 256 | bytes 2048
  205.0 4.5 %copy.97 = bf16[2048,8,64]{0,2,1:T(8,128)(2,1)S(1)} copy(bf16[2048,8,64]{2,1,0:T(8,128)(2,1)} %get-tuple-element.199) | data formatting | bytes 4194304
  210.0 22.5 %fusion.2 = f32[8,8,64,256]{3,2,1,0:T(8,128)} fusion(f32[8,8,256]{2,1,0:T(8,128)S(1)} %add_bitcast_fusion.1, f32[8,256,256]{2,1,0:T(8,128)S(1)} %fusion.33, pred[256,256]{1,0:T(8,128)(4,1)S(1)} %iota_compare_fusion, f32[8,256,8,64]{1,0,3,2:T(8,128)} %get-tuple-element.195), kind=kOutput, calls=%fused_computation.7 | convolution fusion | flops 3238002688 | bytes 10616832 | tf_op jit(solution)/shard_map/khts,kshp->kthp/dot_general | solution.py:99
  232.5 35.1 %while.28 = (s32[]{:T(128)}, f32[8,64,64]{2,1,0:T(8,128)S(1)}, s32[]{:T(128)}, f32[32,8]{1,0:T(8,128)S(1)}, f32[32,8,64,64]{3,2,1,0:T(8,128)}, /*index=5*/s32[]{:T(128)}, s32[]{:T(128)}) while((s32[]{:T(128)}, f32[8,64,64]{2,1,0:T(8,128)S(1)}, s32[]{:T(128)}, f32[32,8]{1,0:T(8,128)S(1)}, f32[32,8,64,64]{3,2,1,0:T(8,128)}, ...), condition=%wide.region_7.8_spmd.clone, body=%wide.region_6.7_spmd.clone.sunk | while | flops 131076 | bytes 393425 | solution.py:34
  232.5 1.1 fusion.55
  233.6 1.1 fusion.55
  234.7 1.1 fusion.55
  235.8 1.1 fusion.55
  236.9 1.1 fusion.55
  238.0 1.1 fusion.55
  239.1 1.1 fusion.55
  240.2 1.1 fusion.55
  241.3 1.1 fusion.55
  242.4 1.1 fusion.55
  243.5 1.1 fusion.55
  244.6 1.1 fusion.55
  245.7 1.1 fusion.55
  246.8 1.1 fusion.55
  247.9 1.1 fusion.55
  249.0 1.1 fusion.55
  250.1 1.1 fusion.55
  251.2 1.1 fusion.55
  252.3 1.1 fusion.55
  253.4 1.1 fusion.55
  254.5 1.1 fusion.55
  255.6 1.1 fusion.55
  256.7 1.1 fusion.55
  257.8 1.1 fusion.55
  258.9 1.1 fusion.55
  260.0 1.1 fusion.55
  261.1 1.1 fusion.55
  262.2 1.1 fusion.55
  263.3 1.1 fusion.55
  264.4 1.1 fusion.55
  265.5 1.1 fusion.55
  266.6 1.1 fusion.55
  267.6 4.9 %fusion.23 = f32[8,8,8,8,256]{4,3,2,1,0:T(8,128)S(1)} fusion(f32[8,8,64,256]{3,2,1,0:T(8,128)} %fusion.2, f32[8,8,64,64]{3,2,1,0:T(8,128)} %get-tuple-element.127, f32[8,256,8]{1,2,0:T(8,128)S(1)} %get-tuple-element.192, f32[8,64,64]{2,1,0:T(8,128)S(1)} %get-tuple-element.129, f32[8,8]{1,0:T(8,128)S(1)} %get-tuple-element.202, ...), kind=kOutput, calls=%fused_computation.39 | convolution fusion | flops 807927808 | bytes 9896192 | tf_op jit(solution)/shard_map/ktn,khpn->kthp/dot_general | solution.py:124
  273.2 1.5 copy-done.3
  274.7 2.9 fusion.27
  277.6 3.3 %all_to_all.35 = bf16[4,512,512]{1,0,2:T(4,128)(2,1)S(1)} reshape(bf16[2048,8,64]{0,2,1:T(8,128)(2,1)} %fusion.27) | data formatting | bytes 4194304 | tf_op jit(solution)/shard_map/all_to_all | solution.py:135
  281.4 27.9 %all_to_all.40 = bf16[4,512,512]{1,2,0:T(8,128)(2,1)S(1)} all-to-all(bf16[4,512,512]{1,2,0:T(8,128)(2,1)S(1)} %copy.88), channel_id=1, replica_groups=mesh['seq'=32,'head'=4] {'head'}, dimensions={0} | all-to-all | bytes 4194304 | tf_op jit(solution)/shard_map/all_to_all | solution.py:135
  310.3 1.1 copy-done.12
  311.4 3.4 %convolution_convert_fusion.1 = bf16[512,1024]{1,0:T(8,128)(2,1)} fusion(bf16[512,2048]{0,1:T(8,128)(2,1)S(1)} %fusion.22, bf16[2048,1024]{1,0:T(8,128)(2,1)S(1)} %copy-done.12), kind=kOutput, calls=%fused_computation.52 | convolution fusion | flops 2148007936 | bytes 7340032 | tf_op jit(solution)/shard_map/dot_general | solution.py:139
  (132 shorter events, 14.1 us)
Async XLA Ops:
  6.5 1.2 copy-start
  11.3 15.6 %all-to-all-start.1 = ((bf16[4,2,2048]{2,1,0:T(2,128)(2,1)}), bf16[4,2,2048]{2,1,0:T(2,128)(2,1)S(1)}, u32[]{:S(2)}, u32[]{:S(2)}) async-start(bf16[4,2,2048]{2,1,0:T(2,128)(2,1)} %reshape.184), calls=%async_computation.1 | async-start | bytes 65536 | tf_op jit(solution)/shard_map/all_to_all | solution.py:68
  26.9 5.1 %copy-start.6 = (f32[4,512]{1,0:T(4,128)S(1)}, f32[4,512]{1,0:T(4,128)}, u32[]{:S(2)}) copy-start(f32[4,512]{1,0:T(4,128)} %param.19) | copy-start | bytes 24580
  26.9 5.2 %copy-start.7 = (f32[4,128]{1,0:T(4,128)S(1)}, f32[4,128]{1,0:T(4,128)}, u32[]{:S(2)}) copy-start(f32[4,128]{1,0:T(4,128)} %param.21) | copy-start | bytes 6148
  26.9 5.2 %copy-start.8 = (f32[512]{0:T(512)S(1)}, f32[512]{0:T(512)}, u32[]{:S(2)}) copy-start(f32[512]{0:T(512)} %param.20) | copy-start | bytes 6148
  26.9 5.2 %copy-start.11 = (f32[128]{0:T(128)S(1)}, f32[128]{0:T(128)}, u32[]{:S(2)}) copy-start(f32[128]{0:T(128)} %param.22) | copy-start | bytes 1540
  26.9 61.9 %copy-start.13 = (f32[8]{0:T(128)S(1)}, f32[8]{0:T(128)}, u32[]{:S(2)}) copy-start(f32[8]{0:T(128)} %param.24) | copy-start | bytes 100
  27.0 62.0 %copy-start.9 = (f32[8]{0:T(128)S(1)}, f32[8]{0:T(128)}, u32[]{:S(2)}) copy-start(f32[8]{0:T(128)} %param.23) | copy-start | bytes 100
  27.0 67.4 %all-to-all-start = ((bf16[512,32,128]{2,0,1:T(8,128)(2,1)}), bf16[512,32,128]{2,0,1:T(8,128)(2,1)}, u32[]{:S(2)}, u32[]{:S(2)}) async-start(bf16[512,32,128]{2,0,1:T(8,128)(2,1)} %bitcast.113), calls=%async_computation | async-start | bytes 8388608 | tf_op jit(solution)/shard_map/all_to_all | solution.py:67
  32.0 200.5 %all-gather.4.cloned.1.call-start = ((), (), s32[]{:S(2)}) async-start(), calls=%async_computation.3 | async-start | bytes 8650752 | tf_op jit(solution)/shard_map/all_gather | solution.py:22
  107.8 2.3 collective-permute-start
  117.1 2.5 copy-start.2
  125.2 7.6 %copy-start.14 = (u32[128]{0:T(128)S(1)}, u32[128]{0:T(128)}, u32[]{:S(2)}) copy-start(u32[128]{0:T(128)} %constant.66) | copy-start | bytes 1540
  132.0 0.7 copy-start.4
  272.5 2.2 copy-start.3
  272.5 2.2 copy-start.10
  281.3 28.4 %copy-start.5 = (f32[2048]{0:T(1024)S(1)}, f32[2048]{0:T(1024)}, u32[]{:S(2)}) copy-start(f32[2048]{0:T(1024)} %param.26) | copy-start | bytes 24580
  309.2 2.2 copy-start.12
  309.7 5.0 %copy-start.1 = (bf16[512,1024]{1,0:T(8,128)(2,1)S(1)}, bf16[512,1024]{1,0:T(8,128)(2,1)}, u32[]{:S(2)}) copy-start(bf16[512,1024]{1,0:T(8,128)(2,1)} %param.16) | copy-start | bytes 3145732
Sparse Core Ops, SparseCore 0:
  132.8 58.4 all-gather.3
where the time goes:
time: 323 us; the launch traced here: 322 us
  blocking collectives  155 us (48%)
  other arithmetic  59.8 us (19%)
  matrix products  43.9 us (14%)
  local copies, waits for them, and re-layouts  35.4 us (11%)
  between operations  14.5 us (4%)
  starting transfers between devices  10.9 us (3%)
    unnamed x1, blocking collectives  70.5 us
    all_gather x1, blocking collectives, on_device(): bc_rows = lax.all_gather(bc_dt[:, :2 * STATE], 'head', axis=0, tiled=True)  56.7 us
    select_n x32, other arithmetic, hop(): return jax.tree.map(lambda a, b: jnp.where(reached, a, b), new, before)  33.7 us
    all_to_all x1, blocking collectives, on_device(): lax.all_to_all(gated_out, 'head', split_axis=0, concat_axis=1, tiled=True)  27.9 us
    dot_general x1, matrix products, on_device(): jnp.einsum('khts,kshp->kthp', mixed, xdt_blocks, precision=highest)  22.5 us
    unnamed x42, local copies, waits for them, and re-layouts  13.7 us
    slice x2, local copies, waits for them, and re-layouts, on_device(): x_chan = gate_x[:, :, HEAD_DIM:].reshape(seq_rows, dinner_here)  8.44 us
    dot_general x1, matrix products, on_device(): jnp.dot(tokens, w_gate_x, preferred_element_type=jnp.float32)  8.12 us
  transfers between devices with their start and end apart: 4, of which 1 were waited for; matrix products, arithmetic and copies ran while one was open for 14% of the time, Pallas kernels for 0%

commit v1 on v0

--- a/solution.py
+++ b/solution.py
@@ -68,7 +68,24 @@
         lax.all_to_all(dt_all, "head", split_axis=1, concat_axis=0, tiled=True),
     )
     dt_raw = dt_raw[:, :, 0]
-    bc_rows = lax.all_gather(bc_dt[:, : 2 * STATE], "head", axis=0, tiled=True)
+    value = bc_dt[:, : 2 * STATE]
+    count_2, index, span = (lax.axis_size("head"), lax.axis_index("head"), value.shape[0])
+    right = [(i_2, (i_2 + 1) % count_2) for i_2 in range(count_2)]
+    behind = [(i_2, (i_2 - 1) % count_2) for i_2 in range(count_2)]
+    bc_rows = jnp.zeros((*value.shape[:0], count_2 * span, *value.shape[0 + 1 :]), value.dtype)
+    bc_rows = lax.dynamic_update_slice_in_dim(bc_rows, value, index * span, axis=0)
+    from_left = from_right = value
+    halfway = count_2 // 2
+    for step in range(1, halfway + 1):
+        from_left = lax.ppermute(from_left, "head", right)
+        bc_rows = lax.dynamic_update_slice_in_dim(
+            bc_rows, from_left, (index - step) % count_2 * span, axis=0
+        )
+        if step < count_2 - halfway:
+            from_right = lax.ppermute(from_right, "head", behind)
+            bc_rows = lax.dynamic_update_slice_in_dim(
+                bc_rows, from_right, (index + step) % count_2 * span, axis=0
+            )
     seq_rows = gate_x.shape[0]
     gate_z = gate_x[:, :, :HEAD_DIM]
     x_chan = gate_x[:, :, HEAD_DIM:].reshape(seq_rows, dinner_here)

time: 323 us -> 319 us (0.988)
  blocking collectives: 155 us -> 98.4 us
  waiting for transfers between devices: 0.77 us -> 49.1 us
  starting transfers between devices: 10.9 us -> 14.3 us
    all_gather x1 -> x0, blocking collectives: 56.7 us -> none  [on_device(): bc_rows = lax.all_gather(bc_dt[:, :2 * STATE], 'head', axis=0, tiled=True)]
    ppermute x0 -> x3, waiting for transfers between devices: none -> 48.3 us  [the longest x2 48.3 us: on_device(): from_left = lax.ppermute(from_left, 'head', right)]
    ppermute x0 -> x3, starting transfers between devices: none -> 3.38 us  [the longest x2 2.13 us: on_device(): from_left = lax.ppermute(from_left, 'head', right)]
  transfers between devices with their start and end apart: 4 -> 7, of which waited for: 1 -> 3; matrix products, arithmetic and copies ran while one was open for 14% -> 14% of each run, Pallas kernels for 0% -> 0%
where the time goes in v1:
time: 319 us; the launch traced here: 317 us
  blocking collectives  98.4 us (31%)
  other arithmetic  59.8 us (19%)
  waiting for transfers between devices  49.1 us (15%)
  matrix products  43.9 us (14%)
  local copies, waits for them, and re-layouts  35.6 us (11%)
  between operations  14.6 us (5%)
  starting transfers between devices  14.3 us (4%)
    unnamed x1, blocking collectives  70.5 us
    ppermute x2, waiting for transfers between devices, on_device(): from_left = lax.ppermute(from_left, 'head', right)  48.3 us
    select_n x32, other arithmetic, hop(): return jax.tree.map(lambda a, b: jnp.where(reached, a, b), new, before)  33.7 us
    all_to_all x1, blocking collectives, on_device(): lax.all_to_all(gated_out, 'head', split_axis=0, concat_axis=1, tiled=True)  28 us
    dot_general x1, matrix products, on_device(): jnp.einsum('khts,kshp->kthp', mixed, xdt_blocks, precision=highest)  22.5 us
    unnamed x42, local copies, waits for them, and re-layouts  13.7 us
    slice x2, local copies, waits for them, and re-layouts, on_device(): x_chan = gate_x[:, :, HEAD_DIM:].reshape(seq_rows, dinner_here)  8.43 us
    dot_general x1, matrix products, on_device(): jnp.dot(tokens, w_gate_x, preferred_element_type=jnp.float32)  8.12 us
  transfers between devices with their start and end apart: 7, of which 3 were waited for; matrix products, arithmetic and copies ran while one was open for 14% of the time, Pallas kernels for 0%

profile of v1, /device:TPU:0, one launch (start us, length us, event | category | flops | bytes accessed | tf_op | source)
XLA Modules:
  0.0 316.8 jit_solution(14234853545892994531)
XLA Ops:
  6.5 1.2 copy-done
  7.8 1.5 convolution_convert_fusion.2
  11.3 4.4 %all-to-all-start.1 = ((bf16[4,2,2048]{2,1,0:T(2,128)(2,1)}), bf16[4,2,2048]{2,1,0:T(2,128)(2,1)S(1)}, u32[]{:S(2)}, u32[]{:S(2)}) async-start(bf16[4,2,2048]{2,1,0:T(2,128)(2,1)} %reshape.184), calls=%async_computation.1 | async-start | bytes 65536 | tf_op jit(solution)/shard_map/all_to_all | solution.py:68
  15.7 8.1 %fusion.28 = bf16[64,32,8,128]{3,2,1,0:T(8,128)(2,1)S(1)} fusion(bf16[512,1024]{1,0:T(8,128)(2,1)S(1)} %copy-done, bf16[1024,4096]{1,0:T(8,128)(2,1)} %param.17), kind=kOutput, calls=%fused_computation.46 | convolution fusion | flops 4297064448 | bytes 13631488 | tf_op jit(solution)/shard_map/dot_general | solution.py:62
  23.8 3.1 copy.126
  27.0 5.0 %all-to-all-start = ((bf16[512,32,128]{2,0,1:T(8,128)(2,1)}), bf16[512,32,128]{2,0,1:T(8,128)(2,1)}, u32[]{:S(2)}, u32[]{:S(2)}) async-start(bf16[512,32,128]{2,0,1:T(8,128)(2,1)} %bitcast.113), calls=%async_computation | async-start | bytes 8388608 | tf_op jit(solution)/shard_map/all_to_all | solution.py:67
  32.1 2.1 collective-permute-start
  34.2 1.2 collective-permute-start.1
  35.8 4.5 %reduce-window.6 = f32[8,8,2,128]{3,1,2,0:T(8,128)S(1)} reduce-window(f32[8,8,2,128]{3,1,2,0:T(8,128)S(1)} %get-tuple-element.196, f32[]{:T(128)} %constant.95.clone.1), window={size=1x1x1x128 pad=0_0x0_0x0_0x127_0}, to_apply=%region_0.1 | reduce-window | flops 2080768 | bytes 131076 | tf_op jit(solution)/shard_map/reduce-window
  41.1 42.2 %collective-permute-done = bf16[512,128]{0,1:T(8,128)(2,1)S(1)} collective-permute-done((bf16[512,128]{0,1:T(8,128)(2,1)S(1)}, bf16[512,128]{0,1:T(8,128)(2,1)S(1)}, u32[]{:S(2)}, u32[]{:S(2)}) %collective-permute-start) | collective-permute-done | bytes 131104 | tf_op jit(solution)/shard_map/ppermute | solution.py:80
  83.3 6.1 %collective-permute-done.2 = bf16[512,128]{0,1:T(8,128)(2,1)S(1)} collective-permute-done((bf16[512,128]{0,1:T(8,128)(2,1)S(1)}, bf16[512,128]{0,1:T(8,128)(2,1)S(1)}, u32[]{:S(2)}, u32[]{:S(2)}) %collective-permute-start.2) | collective-permute-done | bytes 131104 | tf_op jit(solution)/shard_map/ppermute | solution.py:80
  89.4 4.9 %copy.76 = bf16[4,512,8,128]{3,2,1,0:T(8,128)(2,1)S(1)} copy(bf16[4,512,8,128]{3,1,2,0:T(8,128)(2,1)} %bitcast.2) | data formatting | bytes 8388608 | tf_op jit(solution)/shard_map/all_to_all | solution.py:67
  94.3 4.0 %fusion.44 = (bf16[2048,8,64]{2,1,0:T(8,128)(2,1)}, bf16[2048,8,64]{2,1,0:T(8,128)(2,1)}) fusion(bf16[2048,8,128]{2,1,0:T(8,128)(2,1)S(1)} %bitcast.109), kind=kLoop, calls=%fused_computation.91 | loop fusion | bytes 8388608 | tf_op jit(solution)/shard_map/slice | solution.py:91
  98.3 4.5 %copy.77 = bf16[2048,8,64]{0,2,1:T(8,128)(2,1)S(1)} copy(bf16[2048,8,64]{2,1,0:T(8,128)(2,1)} %get-tuple-element.198) | data formatting | bytes 4194304 | tf_op jit(solution)/shard_map/slice | solution.py:91
  102.9 1.5 collective-permute-start.3
  105.2 1.1 maximum_convert_fusion
  106.4 5.2 %multiply_convert_fusion = bf16[2048,640]{0,1:T(8,128)(2,1)S(1)} fusion(f32[2051,640]{0,1:T(8,128)S(1)} %maximum_convert_fusion, f32[640]{0:T(1024)S(1)} %get-tuple-element.169, f32[640]{0:T(1024)S(1)} %get-tuple-element.170, f32[640]{0:T(1024)S(1)} %get-tuple-element.171, f32[640]{0:T(1024)S(1)} %get-tuple-element.168, f32[640]{0:T(1024)S(1)} %pad_maximum_fusion.1), kind=kLoop, calls=%fused_computation.29 | loop fusion | flops 17039360 | bytes 23605760 | tf_op jit(solution)/shard_map/convert_element_type | solution.py:41
  112.2 2.0 copy.105
  114.7 2.5 broadcast_multiply_fusion
  117.2 3.0 fusion.24
  120.2 6.8 %while.27 = (s32[]{:T(128)}, f32[8,64,64]{2,1,0:T(8,128)S(1)}, f32[8,8,64,64]{3,2,1,0:T(8,128)}, f32[8,8]{1,0:T(8,128)S(1)}, f32[8,8,64,64]{3,2,1,0:T(8,128)S(1)}, /*index=5*/s32[]{:T(128)}, s32[]{:T(128)}) while((s32[]{:T(128)}, f32[8,64,64]{2,1,0:T(8,128)S(1)}, f32[8,8,64,64]{3,2,1,0:T(8,128)}, f32[8,8]{1,0:T(8,128)S(1)}, ...), condition=%wide.region_3.4_spmd.clone, body=%wide.region_2.3_spmd.clone.sunk | while | flops 131075 | bytes 786636 | solution.py:128
  129.4 70.5 %all-reduce = f32[256]{0:T(256)S(1)} all-reduce(f32[256]{0:T(256)S(1)} %dynamic-update-slice), channel_id=2, replica_groups=mesh['seq'=32,'head'=4] {'seq'}, use_global_device_ids=true, to_apply=%add | all-reduce | flops 256 | bytes 2048
  200.0 4.5 %copy.100 = bf16[2048,8,64]{0,2,1:T(8,128)(2,1)S(1)} copy(bf16[2048,8,64]{2,1,0:T(8,128)(2,1)} %get-tuple-element.199) | data formatting | bytes 4194304
  205.1 22.5 %fusion.2 = f32[8,8,64,256]{3,2,1,0:T(8,128)} fusion(f32[8,8,256]{2,1,0:T(8,128)S(1)} %add_bitcast_fusion.1, f32[8,256,256]{2,1,0:T(8,128)S(1)} %fusion.33, pred[256,256]{1,0:T(8,128)(4,1)S(1)} %iota_compare_fusion, f32[8,256,8,64]{1,0,3,2:T(8,128)} %get-tuple-element.195), kind=kOutput, calls=%fused_computation.7 | convolution fusion | flops 3238002688 | bytes 10616832 | tf_op jit(solution)/shard_map/khts,kshp->kthp/dot_general | solution.py:116
  227.6 35.1 %while.28 = (s32[]{:T(128)}, f32[8,64,64]{2,1,0:T(8,128)S(1)}, s32[]{:T(128)}, f32[32,8]{1,0:T(8,128)S(1)}, f32[32,8,64,64]{3,2,1,0:T(8,128)}, /*index=5*/s32[]{:T(128)}, s32[]{:T(128)}) while((s32[]{:T(128)}, f32[8,64,64]{2,1,0:T(8,128)S(1)}, s32[]{:T(128)}, f32[32,8]{1,0:T(8,128)S(1)}, f32[32,8,64,64]{3,2,1,0:T(8,128)}, ...), condition=%wide.region_7.8_spmd.clone, body=%wide.region_6.7_spmd.clone.sunk | while | flops 131076 | bytes 393425 | solution.py:34
  227.6 1.1 fusion.56
  228.7 1.1 fusion.56
  229.8 1.1 fusion.56
  230.9 1.1 fusion.56
  232.0 1.1 fusion.56
  233.1 1.1 fusion.56
  234.2 1.1 fusion.56
  235.3 1.1 fusion.56
  236.4 1.1 fusion.56
  237.5 1.1 fusion.56
  238.6 1.1 fusion.56
  239.7 1.1 fusion.56
  240.8 1.1 fusion.56
  241.9 1.1 fusion.56
  243.0 1.1 fusion.56
  244.1 1.1 fusion.56
  245.2 1.1 fusion.56
  246.3 1.1 fusion.56
  247.4 1.1 fusion.56
  248.5 1.1 fusion.56
  249.6 1.1 fusion.56
  250.7 1.1 fusion.56
  251.8 1.1 fusion.56
  252.9 1.1 fusion.56
  254.0 1.1 fusion.56
  255.1 1.1 fusion.56
  256.2 1.1 fusion.56
  257.3 1.1 fusion.56
  258.4 1.1 fusion.56
  259.5 1.1 fusion.56
  260.6 1.1 fusion.56
  261.7 1.1 fusion.56
  262.7 4.9 %fusion.23 = f32[8,8,8,8,256]{4,3,2,1,0:T(8,128)S(1)} fusion(f32[8,8,64,256]{3,2,1,0:T(8,128)} %fusion.2, f32[8,8,64,64]{3,2,1,0:T(8,128)} %get-tuple-element.127, f32[8,256,8]{1,2,0:T(8,128)S(1)} %get-tuple-element.192, f32[8,64,64]{2,1,0:T(8,128)S(1)} %get-tuple-element.129, f32[8,8]{1,0:T(8,128)S(1)} %get-tuple-element.204, ...), kind=kOutput, calls=%fused_computation.39 | convolution fusion | flops 807927808 | bytes 9896192 | tf_op jit(solution)/shard_map/ktn,khpn->kthp/dot_general | solution.py:141
  268.3 1.5 copy-done.3
  269.8 2.9 fusion.27
  272.7 3.3 %all_to_all.35 = bf16[4,512,512]{1,0,2:T(4,128)(2,1)S(1)} reshape(bf16[2048,8,64]{0,2,1:T(8,128)(2,1)} %fusion.27) | data formatting | bytes 4194304 | tf_op jit(solution)/shard_map/all_to_all | solution.py:152
  276.4 28.0 %all_to_all.40 = bf16[4,512,512]{1,2,0:T(8,128)(2,1)S(1)} all-to-all(bf16[4,512,512]{1,2,0:T(8,128)(2,1)S(1)} %copy.91), channel_id=1, replica_groups=mesh['seq'=32,'head'=4] {'head'}, dimensions={0} | all-to-all | bytes 4194304 | tf_op jit(solution)/shard_map/all_to_all | solution.py:152
  305.5 1.1 copy-done.12
  306.6 3.4 %convolution_convert_fusion.1 = bf16[512,1024]{1,0:T(8,128)(2,1)} fusion(bf16[512,2048]{0,1:T(8,128)(2,1)S(1)} %fusion.22, bf16[2048,1024]{1,0:T(8,128)(2,1)S(1)} %copy-done.12), kind=kOutput, calls=%fused_computation.52 | convolution fusion | flops 2148007936 | bytes 7340032 | tf_op jit(solution)/shard_map/dot_general | solution.py:156
  (141 shorter events, 16.6 us)
Async XLA Ops:
  6.5 1.2 copy-start
  11.3 15.6 %all-to-all-start.1 = ((bf16[4,2,2048]{2,1,0:T(2,128)(2,1)}), bf16[4,2,2048]{2,1,0:T(2,128)(2,1)S(1)}, u32[]{:S(2)}, u32[]{:S(2)}) async-start(bf16[4,2,2048]{2,1,0:T(2,128)(2,1)} %reshape.184), calls=%async_computation.1 | async-start | bytes 65536 | tf_op jit(solution)/shard_map/all_to_all | solution.py:68
  26.9 8.6 %copy-start.6 = (f32[4,512]{1,0:T(4,128)S(1)}, f32[4,512]{1,0:T(4,128)}, u32[]{:S(2)}) copy-start(f32[4,512]{1,0:T(4,128)} %param.19) | copy-start | bytes 24580
  26.9 8.6 %copy-start.7 = (f32[4,128]{1,0:T(4,128)S(1)}, f32[4,128]{1,0:T(4,128)}, u32[]{:S(2)}) copy-start(f32[4,128]{1,0:T(4,128)} %param.21) | copy-start | bytes 6148
  26.9 8.6 %copy-start.8 = (f32[512]{0:T(512)S(1)}, f32[512]{0:T(512)}, u32[]{:S(2)}) copy-start(f32[512]{0:T(512)} %param.20) | copy-start | bytes 6148
  26.9 8.6 %copy-start.11 = (f32[128]{0:T(128)S(1)}, f32[128]{0:T(128)}, u32[]{:S(2)}) copy-start(f32[128]{0:T(128)} %param.22) | copy-start | bytes 1540
  26.9 8.6 %copy-start.13 = (f32[8]{0:T(128)S(1)}, f32[8]{0:T(128)}, u32[]{:S(2)}) copy-start(f32[8]{0:T(128)} %param.24) | copy-start | bytes 100
  27.0 8.7 %copy-start.9 = (f32[8]{0:T(128)S(1)}, f32[8]{0:T(128)}, u32[]{:S(2)}) copy-start(f32[8]{0:T(128)} %param.23) | copy-start | bytes 100
  27.0 62.5 %all-to-all-start = ((bf16[512,32,128]{2,0,1:T(8,128)(2,1)}), bf16[512,32,128]{2,0,1:T(8,128)(2,1)}, u32[]{:S(2)}, u32[]{:S(2)}) async-start(bf16[512,32,128]{2,0,1:T(8,128)(2,1)} %bitcast.113), calls=%async_computation | async-start | bytes 8388608 | tf_op jit(solution)/shard_map/all_to_all | solution.py:67
  32.0 195.6 %all-gather.4.cloned.1.call-start = ((), (), s32[]{:S(2)}) async-start(), calls=%async_computation.3 | async-start | bytes 8650752 | tf_op jit(solution)/shard_map/all_gather | solution.py:22
  32.1 51.1 %collective-permute-start = (bf16[512,128]{0,1:T(8,128)(2,1)S(1)}, bf16[512,128]{0,1:T(8,128)(2,1)S(1)}, u32[]{:S(2)}, u32[]{:S(2)}) collective-permute-start(bf16[512,128]{0,1:T(8,128)(2,1)S(1)} %get-tuple-element.202), channel_id=1, source_target_pairs={{0,1},{1,2},{2,3},{3,0},{4,5},{5,6},{6,7},{7,4},{8,9},{9,10},{10,1... | collective-permute-start | bytes 393224 | tf_op jit(solution)/shard_map/ppermute | solution.py:80
  34.2 49.0 %collective-permute-start.1 = (bf16[512,128]{0,1:T(8,128)(2,1)S(1)}, bf16[512,128]{0,1:T(8,128)(2,1)S(1)}, u32[]{:S(2)}, u32[]{:S(2)}) collective-permute-start(bf16[512,128]{0,1:T(8,128)(2,1)S(1)} %get-tuple-element.202), channel_id=1, source_target_pairs={{0,3},{1,0},{2,1},{3,2},{4,7},{5,4},{6,5},{7,6},{8,11},{9,8},{10,9... | collective-permute-start | bytes 393224 | tf_op jit(solution)/shard_map/ppermute | solution.py:85
  83.2 6.2 %collective-permute-start.2 = (bf16[512,128]{0,1:T(8,128)(2,1)S(1)}, bf16[512,128]{0,1:T(8,128)(2,1)S(1)}, u32[]{:S(2)}, u32[]{:S(2)}) collective-permute-start(bf16[512,128]{0,1:T(8,128)(2,1)S(1)} %collective-permute-done), channel_id=1, source_target_pairs={{0,1},{1,2},{2,3},{3,0},{4,5},{5,6},{6,7},{7,4},{8,9},{9,10},{10,1... | collective-permute-start | bytes 393224 | tf_op jit(solution)/shard_map/ppermute | solution.py:80
  102.9 2.3 collective-permute-start.3
  112.2 2.5 copy-start.2
  120.2 7.6 %copy-start.14 = (u32[128]{0:T(128)S(1)}, u32[128]{0:T(128)}, u32[]{:S(2)}) copy-start(u32[128]{0:T(128)} %constant.102) | copy-start | bytes 1540
  127.0 0.7 copy-start.4
  267.6 2.2 copy-start.3
  267.6 2.2 copy-start.10
  276.4 28.5 %copy-start.5 = (f32[2048]{0:T(1024)S(1)}, f32[2048]{0:T(1024)}, u32[]{:S(2)}) copy-start(f32[2048]{0:T(1024)} %param.26) | copy-start | bytes 24580
  304.4 2.2 copy-start.12
  305.0 5.0 %copy-start.1 = (bf16[512,1024]{1,0:T(8,128)(2,1)S(1)}, bf16[512,1024]{1,0:T(8,128)(2,1)}, u32[]{:S(2)}) copy-start(bf16[512,1024]{1,0:T(8,128)(2,1)} %param.16) | copy-start | bytes 3145732
Sparse Core Ops, SparseCore 0:
  127.9 57.4 all-gather.3
